TPU v7x, 1024 devices: a whole 4x8x16 slice. The times are simulated.
1024 devices in a mesh: pipe: 8 (over y), dp: 32 (over z, core), tensor: 4 (over x).
Axes of the slice: x: 4, y: 8, z: 16, core: 2. Of those that a mesh axis runs over, the one named last changes fastest.
Arguments:
- activations: bfloat16 [8, 2, 4096, 16384], P('pipe', None, 'dp', 'tensor'), may hold values from -6 to 6
- cotangent: bfloat16 [8, 2, 4096, 1024], P('pipe', None, 'dp', 'tensor'), may hold values from -0.5 to 0.5
- error_tiles: bfloat16 [8, 32, 4, 4, 4, 128, 128], P('pipe', 'dp', 'tensor'), may hold values from -4 to 4
- tile_picks: int32 [8, 32, 4, 4, 4, 2], P('pipe', None, 'tensor'), may hold values from 0 to 31, as said below
- row_owners: int32 [8, 4, 32], P('pipe', 'tensor'), may hold values from 0 to 31, as said below
Outputs:
- grad_strips: bfloat16 [8, 4, 4096, 1024], P('pipe', 'tensor', 'dp')
Inputs may be any that keep to these rules, and one draw needn't show every extreme that they name: `tile_picks`: for each section, replica and row group, the 16 picked row blocks j have distinct owners row_owners[p, u, j]; c is below 2. Each row_owners[p, u] is a permutation of 0 to 31.
All inputs are finite; a program needn't handle non-finite values.
Results may differ from a plain program's by a relative error of at most 0.001.
Values may be sent and summed in bfloat16 or wider, within the bound.
A program may use at most 32 MiB of HBM per device.

v0:
```python
import jax
import jax.numpy as jnp
from jax import lax
from jax.sharding import PartitionSpec as P


def passed_along(value, axis, steps):
    count = lax.axis_size(axis)
    pairs = [(source, (source + steps) % count) for source in range(count)]
    return lax.ppermute(value, axis, pairs)


def body(activations, cotangent, error_tiles, tile_picks, row_owners):
    tile_edge = error_tiles.shape[-1]
    tensor_count = lax.axis_size("tensor")
    replica_count = lax.axis_size("dp")
    replica_index = lax.axis_index("dp")
    returned = passed_along(cotangent, "pipe", -1)
    columns = lax.all_gather(returned, "tensor", axis=3, tiled=True)
    arrived = lax.all_to_all(error_tiles, "tensor", split_axis=3, concat_axis=2, tiled=True)
    width = columns.shape[-1]
    col_blocks = width // tile_edge
    group_blocks = col_blocks // tensor_count
    local_rows = activations.shape[-1] // tile_edge
    owned = local_rows // replica_count
    token_rows = activations.shape[1] * activations.shape[2]
    inputs = activations.reshape(token_rows, local_rows, tile_edge)
    outputs = columns.reshape(token_rows, col_blocks, tile_edge)
    every_pick = tile_picks[0, :, 0]
    source_offset = (jnp.arange(tensor_count, dtype=jnp.int32) * group_blocks)[None, :, None]
    pick_rows = every_pick[..., 0].reshape(replica_count, -1)
    pick_cols = (every_pick[..., 1] + source_offset).reshape(replica_count, -1)
    mine_rows = lax.dynamic_index_in_dim(pick_rows, replica_index, 0, keepdims=False)
    mine_cols = lax.dynamic_index_in_dim(pick_cols, replica_index, 0, keepdims=False)
    picked_in = jnp.take(inputs, mine_rows, axis=1)
    picked_out = jnp.take(outputs, mine_cols, axis=1)
    slot_total = mine_rows.shape[0]
    grads = jnp.einsum("tmi,tmk->mik", picked_in, picked_out, preferred_element_type=jnp.float32)
    grads = grads.reshape(slot_total, tile_edge * tile_edge)
    table = row_owners[0, 0]
    placed = jnp.sum(
        jnp.where(pick_rows[..., None] == jnp.arange(local_rows, dtype=jnp.int32), table, 0),
        axis=-1,
    )
    owner_index = placed // owned
    within_owner = placed % owned
    my_owner = lax.dynamic_index_in_dim(owner_index, replica_index, 0, keepdims=False)
    send_map = (my_owner[None, :] == jnp.arange(replica_count, dtype=jnp.int32)[:, None]).astype(
        jnp.float32
    )
    position = within_owner * col_blocks + pick_cols
    landing = (owner_index == replica_index)[..., None] & (
        position[..., None] == jnp.arange(owned * col_blocks, dtype=jnp.int32)
    )
    recv_map = jnp.transpose(jnp.sum(landing.astype(jnp.float32), axis=1))
    carried = arrived.reshape(slot_total, tile_edge * tile_edge).astype(jnp.float32)
    highest = lax.Precision.HIGHEST
    outgoing = jnp.dot(
        send_map, grads + carried, precision=highest, preferred_element_type=jnp.float32
    )
    incoming = lax.all_to_all(outgoing, "dp", split_axis=0, concat_axis=0, tiled=True)
    strip = jnp.dot(recv_map, incoming, precision=highest, preferred_element_type=jnp.float32)
    strip = strip.reshape(owned, col_blocks, tile_edge, tile_edge)
    strip = jnp.transpose(strip, (0, 2, 1, 3)).reshape(1, 1, owned * tile_edge, width)
    return strip.astype(jnp.bfloat16)


def solution(mesh):
    in_specs = (
        P("pipe", None, "dp", "tensor"),
        P("pipe", None, "dp", "tensor"),
        P("pipe", "dp", "tensor", None, None, None, None),
        P("pipe", None, "tensor", None, None, None),
        P("pipe", "tensor", None),
    )
    out_specs = P("pipe", "tensor", "dp", None)
    return jax.shard_map(body, mesh=mesh, in_specs=in_specs, out_specs=out_specs, check_vma=False)
```

profile of v0, /device:TPU:1, one launch (start us, length us, event | category | flops | bytes accessed | tf_op | source)
XLA Modules:
  0.0 162.4 jit_solution(9093283139533421780)
XLA Ops:
  0.0 5.9 %collective-permute-start = (bf16[1,2,128,256]{3,2,1,0:T(8,128)(2,1)}, bf16[1,2,128,256]{3,2,1,0:T(8,128)(2,1)S(1)}, u32[]{:S(2)}, u32[]{:S(2)}) collective-permute-start(bf16[1,2,128,256]{3,2,1,0:T(8,128)(2,1)} %param.6), channel_id=1, source_target_pairs={{0,896},{128,0},{256,128},{384,256},{512,384},{640,512},{768,640},... | collective-permute-start | bytes 393224 | tf_op jit(solution)/shard_map/ppermute | solution.py:10
  5.9 4.0 %all-to-all-start = ((bf16[1,1,1,4,4,128,128]{6,5,4,2,1,0,3:T(8,128)(2,1)}), bf16[1,1,1,4,4,128,128]{6,5,4,2,1,0,3:T(8,128)(2,1)S(1)}, u32[]{:S(2)}, u32[]{:S(2)}) async-start(bf16[1,1,1,4,4,128,128]{6,5,4,2,1,0,3:T(8,128)(2,1)} %bitcast.75), calls=%async_computation | async-start | bytes 1048576 | tf_op jit(solution)/shard_map/all_to_all | solution.py:20
  9.9 0.8 fusion.27
  10.8 0.1 add.68
  10.8 0.1 add.69
  10.9 0.1 copy.60
  11.0 0.1 broadcast_add_fusion
  11.1 0.2 dynamic-slice_reduce_fusion
  11.3 1.4 select_reduce_fusion
  12.7 2.1 %copy.72 = bf16[32,8,32,128]{3,2,1,0:T(8,128)(2,1)S(1)} copy(bf16[32,8,32,128]{3,1,2,0:T(8,128)(2,1)} %bitcast.72) | data formatting | bytes 4194304
  14.8 0.8 copy.63
  15.6 1.7 %gather_fusion = bf16[16,256,128]{2,1,0:T(8,128)(2,1)} fusion(bf16[256,32,128]{2,0,1:T(8,128)(2,1)S(1)} %copy.63, s32[1024]{0:T(1024)S(1)} %pad_clamp_fusion.1), kind=kCustom, calls=%fused_computation | custom fusion | bytes 2097216 | tf_op jit(solution)/shard_map/jit(_take)/gather | solution.py:35
  17.3 11.8 %all_gather.3 = bf16[1,2,128,1024]{3,2,1,0:T(8,128)(2,1)S(1)} all-gather(bf16[1,2,128,256]{3,2,1,0:T(8,128)(2,1)S(1)} %collective-permute-done), channel_id=1, replica_groups=mesh['pipe'=8,'dp'=32,'tensor'=4] {'tensor'}, dimensions={3}, use_global_device_ids=true | all-gather | bytes 655360 | tf_op jit(solution)/shard_map/all_gather | solution.py:19
  29.1 0.1 copy.73
  29.2 0.1 copy.64
  29.2 1.7 %gather_fusion.1 = bf16[16,256,128]{2,1,0:T(8,128)(2,1)} fusion(bf16[256,8,128]{2,0,1:T(8,128)(2,1)S(1)} %copy.64, s32[1024]{0:T(1024)S(1)} %pad_clamp_fusion), kind=kCustom, calls=%fused_computation.1 | custom fusion | bytes 2097216 | tf_op jit(solution)/shard_map/jit(_take)/gather | solution.py:36
  30.9 1.8 %fusion.12 = f32[16,128,128]{2,1,0:T(8,128)S(1)} fusion(bf16[16,256,128]{2,1,0:T(8,128)(2,1)} %gather_fusion.1, bf16[16,256,128]{2,1,0:T(8,128)(2,1)S(1)} %copy-done, pred[16]{0:T(512)(128)(4,1)S(1)} %get-tuple-element.7, pred[16]{0:T(512)(128)(4,1)S(1)} %get-tuple-element.8), kind=kOutput, calls=%fused_computation.13 | convolution fusion | flops 135266304 | bytes 3145760 | tf_op jit(solution)/shard_map/tmi,tmk->mik/dot_general | solution.py:38
  32.7 0.1 convert.3
  32.8 2.3 %convolution_bitcast_fusion = f32[32,1,16384]{2,0,1:T(8,128)S(1)} fusion(f32[2,8,128,128]{3,2,1,0:T(8,128)S(1)} %convert.3, f32[2,8,128,128]{3,2,1,0:T(8,128)S(1)} %bitcast.74, s32[16]{0:T(128)S(1)} %fusion.23), kind=kOutput, calls=%fused_computation.2 | convolution fusion | flops 100925952 | bytes 4194368 | tf_op jit(solution)/shard_map/dot_general | solution.py:58
  35.1 3.5 %copy.67 = f32[32,1,16384]{2,1,0:T(1,128)} copy(f32[32,1,16384]{2,0,1:T(8,128)S(1)} %convolution_bitcast_fusion) | data formatting | bytes 4194304 | tf_op jit(solution)/shard_map/all_to_all | solution.py:61
  38.6 22.4 %all-to-all-start.1 = ((f32[32,1,16384]{2,1,0:T(1,128)}), f32[32,1,16384]{2,1,0:T(1,128)S(1)}, u32[]{:S(2)}, u32[]{:S(2)}) async-start(f32[32,1,16384]{2,1,0:T(1,128)} %copy.67), calls=%async_computation.1 | async-start | bytes 4194304 | tf_op jit(solution)/shard_map/all_to_all | solution.py:61
  61.1 98.2 %all-to-all-done.1 = f32[32,1,16384]{2,1,0:T(1,128)S(1)} async-done(((f32[32,1,16384]{2,1,0:T(1,128)}), f32[32,1,16384]{2,1,0:T(1,128)S(1)}, u32[]{:S(2)}, u32[]{:S(2)}) %all-to-all-start.1) | async-done | bytes 2097184 | tf_op jit(solution)/shard_map/all_to_all | solution.py:61
  159.3 2.2 %fusion.6 = bf16[1,128,8,128]{3,2,1,0:T(8,128)(2,1)S(1)} fusion(f32[32,8]{0,1:T(8,128)S(1)} %convert_reduce_fusion, f32[32,1,16384]{2,1,0:T(1,128)S(1)} %all-to-all-done.1), kind=kOutput, calls=%fused_computation.8 | convolution fusion | flops 50462720 | bytes 2360320 | tf_op jit(solution)/shard_map/dot_general | solution.py:62
  161.5 0.8 convert_element_type.36
  (13 shorter events, 0.2 us)
Async XLA Ops:
  0.0 17.3 %collective-permute-start = (bf16[1,2,128,256]{3,2,1,0:T(8,128)(2,1)}, bf16[1,2,128,256]{3,2,1,0:T(8,128)(2,1)S(1)}, u32[]{:S(2)}, u32[]{:S(2)}) collective-permute-start(bf16[1,2,128,256]{3,2,1,0:T(8,128)(2,1)} %param.6), channel_id=1, source_target_pairs={{0,896},{128,0},{256,128},{384,256},{512,384},{640,512},{768,640},... | collective-permute-start | bytes 393224 | tf_op jit(solution)/shard_map/ppermute | solution.py:10
  5.9 26.8 %all-to-all-start = ((bf16[1,1,1,4,4,128,128]{6,5,4,2,1,0,3:T(8,128)(2,1)}), bf16[1,1,1,4,4,128,128]{6,5,4,2,1,0,3:T(8,128)(2,1)S(1)}, u32[]{:S(2)}, u32[]{:S(2)}) async-start(bf16[1,1,1,4,4,128,128]{6,5,4,2,1,0,3:T(8,128)(2,1)} %bitcast.75), calls=%async_computation | async-start | bytes 1048576 | tf_op jit(solution)/shard_map/all_to_all | solution.py:20
  29.1 1.9 %copy-start = (bf16[16,256,128]{2,1,0:T(8,128)(2,1)S(1)}, bf16[16,256,128]{2,1,0:T(8,128)(2,1)}, u32[]{:S(2)}) copy-start(bf16[16,256,128]{2,1,0:T(8,128)(2,1)} %gather_fusion) | copy-start | bytes 3145732
  38.6 120.7 %all-to-all-start.1 = ((f32[32,1,16384]{2,1,0:T(1,128)}), f32[32,1,16384]{2,1,0:T(1,128)S(1)}, u32[]{:S(2)}, u32[]{:S(2)}) async-start(f32[32,1,16384]{2,1,0:T(1,128)} %copy.67), calls=%async_computation.1 | async-start | bytes 4194304 | tf_op jit(solution)/shard_map/all_to_all | solution.py:61
where the time goes:
time: 163 us; the launch traced here: 162 us
  waiting for transfers between devices  98.2 us (60%)
  starting transfers between devices  32.3 us (20%)
  local copies, waits for them, and re-layouts  12 us (7%)
  blocking collectives  11.8 us (7%)
  matrix products  6.32 us (4%)
    all_to_all x1, waiting for transfers between devices, body(): lax.all_to_all(outgoing, 'dp', split_axis=0, concat_axis=0, tiled=True)  98.2 us
    all_to_all x1, starting transfers between devices, body(): lax.all_to_all(outgoing, 'dp', split_axis=0, concat_axis=0, tiled=True)  22.4 us
    all_gather x1, blocking collectives, body(): columns = lax.all_gather(returned, 'tensor', axis=3, tiled=True)  11.8 us
    ppermute x1, starting transfers between devices, passed_along(): return lax.ppermute(value, axis, pairs)  5.9 us
    all_to_all x1, starting transfers between devices, body(): lax.all_to_all(error_tiles, 'tensor', split_axis=3, concat_axis=2, tiled=...  4.02 us
    all_to_all x1, local copies, waits for them, and re-layouts, body(): lax.all_to_all(outgoing, 'dp', split_axis=0, concat_axis=0, tiled=True)  3.5 us
  transfers between devices with their start and end apart: 3, of which 1 were waited for; matrix products, arithmetic and copies ran while one was open for 7% of the time, Pallas kernels for 0%

commit v1 on v0

--- a/solution.py
+++ b/solution.py
@@ -58,7 +58,15 @@
     outgoing = jnp.dot(
         send_map, grads + carried, precision=highest, preferred_element_type=jnp.float32
     )
-    incoming = lax.all_to_all(outgoing, "dp", split_axis=0, concat_axis=0, tiled=True)
+    outgoing = outgoing.reshape(replica_count, tile_edge, tile_edge)
+    levels = 32767.0
+    reach = jnp.maximum(jnp.max(jnp.abs(outgoing), axis=1, keepdims=True), 1e-30)
+    codes = jnp.round(outgoing * (levels / reach)).astype(jnp.int16)
+    codes = lax.all_to_all(codes, "dp", split_axis=0, concat_axis=0, tiled=True)
+    steps = lax.all_to_all(
+        reach * (1.0 / levels), "dp", split_axis=0, concat_axis=0, tiled=True
+    )
+    incoming = (codes.astype(jnp.float32) * steps).reshape(replica_count, -1)
     strip = jnp.dot(recv_map, incoming, precision=highest, preferred_element_type=jnp.float32)
     strip = strip.reshape(owned, col_blocks, tile_edge, tile_edge)
     strip = jnp.transpose(strip, (0, 2, 1, 3)).reshape(1, 1, owned * tile_edge, width)

time: 163 us -> 134 us (0.82)
  waiting for transfers between devices: 98.2 us -> 65.7 us
  starting transfers between devices: 32.3 us -> 36.7 us
    all_to_all x1 -> x2, waiting for transfers between devices: 98.2 us -> 65.7 us  [the longest x1 55.7 us: body(): codes = lax.all_to_all(codes, 'dp', split_axis=0, concat_axis=0, tiled=True)]
    all_to_all x1 -> x2, starting transfers between devices: 22.4 us -> 26.7 us  [the longest x1 22.3 us: body(): lax.all_to_all(reach * (1.0 / levels), 'dp', split_axis=0, concat_axis=0,...]
    all_to_all x1 -> x0, local copies, waits for them, and re-layouts: 3.5 us -> none  [body(): lax.all_to_all(outgoing, 'dp', split_axis=0, concat_axis=0, tiled=True)]
    unnamed x4 -> x6, local copies, waits for them, and re-layouts: 2.17 us -> 3.57 us
  transfers between devices with their start and end apart: 3 -> 4, of which waited for: 1 -> 2; matrix products, arithmetic and copies ran while one was open for 7% -> 9% of each run, Pallas kernels for 0% -> 0%
where the time goes in v1:
time: 134 us
  waiting for transfers between devices  65.7 us (49%)
  starting transfers between devices  36.7 us (27%)
  blocking collectives  11.9 us (9%)
  local copies, waits for them, and re-layouts  10.4 us (8%)
  matrix products  6.1 us (5%)
  other arithmetic  2.93 us (2%)
    all_to_all x1, waiting for transfers between devices, body(): codes = lax.all_to_all(codes, 'dp', split_axis=0, concat_axis=0, tiled=True)  55.7 us
    all_to_all x1, starting transfers between devices, body(): lax.all_to_all(reach * (1.0 / levels), 'dp', split_axis=0, concat_axis=0,...  22.3 us
    all_gather x1, blocking collectives, body(): columns = lax.all_gather(returned, 'tensor', axis=3, tiled=True)  11.9 us
    all_to_all x1, waiting for transfers between devices, body(): lax.all_to_all(reach * (1.0 / levels), 'dp', split_axis=0, concat_axis=0,...  10 us
    ppermute x1, starting transfers between devices, passed_along(): return lax.ppermute(value, axis, pairs)  5.9 us
    all_to_all x1, starting transfers between devices, body(): codes = lax.all_to_all(codes, 'dp', split_axis=0, concat_axis=0, tiled=True)  4.49 us
    all_to_all x1, starting transfers between devices, body(): lax.all_to_all(error_tiles, 'tensor', split_axis=3, concat_axis=2, tiled=...  4.02 us
    unnamed x6, local copies, waits for them, and re-layouts  3.57 us
  transfers between devices with their start and end apart: 4, of which 2 were waited for; matrix products, arithmetic and copies ran while one was open for 9% of the time, Pallas kernels for 0%

profile of v1, /device:TPU:1, one launch (start us, length us, event | category | flops | bytes accessed | tf_op | source)
XLA Modules:
  0.0 133.7 jit_solution(9545247856726495201)
XLA Ops:
  0.0 5.9 %collective-permute-start = (bf16[1,2,128,256]{3,2,1,0:T(8,128)(2,1)}, bf16[1,2,128,256]{3,2,1,0:T(8,128)(2,1)S(1)}, u32[]{:S(2)}, u32[]{:S(2)}) collective-permute-start(bf16[1,2,128,256]{3,2,1,0:T(8,128)(2,1)} %param.6), channel_id=1, source_target_pairs={{0,896},{128,0},{256,128},{384,256},{512,384},{640,512},{768,640},... | collective-permute-start | bytes 393224 | tf_op jit(solution)/shard_map/ppermute | solution.py:10
  5.9 4.0 %all-to-all-start = ((bf16[1,1,1,4,4,128,128]{6,5,4,2,1,0,3:T(8,128)(2,1)}), bf16[1,1,1,4,4,128,128]{6,5,4,2,1,0,3:T(8,128)(2,1)S(1)}, u32[]{:S(2)}, u32[]{:S(2)}) async-start(bf16[1,1,1,4,4,128,128]{6,5,4,2,1,0,3:T(8,128)(2,1)} %bitcast.96), calls=%async_computation | async-start | bytes 1048576 | tf_op jit(solution)/shard_map/all_to_all | solution.py:20
  9.9 0.8 fusion.30
  11.1 0.2 dynamic-slice_reduce_fusion
  11.3 1.4 %select_reduce_fusion = s32[32,16]{1,0:T(8,128)S(1)} fusion(s32[32]{0:T(128)} %bitcast.101, s32[32,16]{1,0:T(8,128)S(1)} %copy.58), kind=kLoop, calls=%fused_computation.24 | loop fusion | flops 48640 | bytes 4224 | tf_op jit(solution)/shard_map/reduce_sum | solution.py:41
  12.7 2.1 %copy.71 = bf16[32,8,32,128]{3,2,1,0:T(8,128)(2,1)S(1)} copy(bf16[32,8,32,128]{3,1,2,0:T(8,128)(2,1)} %bitcast.93) | data formatting | bytes 4194304
  14.8 0.8 copy.61
  15.6 1.7 %gather_fusion = bf16[16,256,128]{2,1,0:T(8,128)(2,1)} fusion(bf16[256,32,128]{2,0,1:T(8,128)(2,1)S(1)} %copy.61, s32[1024]{0:T(1024)S(1)} %pad_clamp_fusion.1), kind=kCustom, calls=%fused_computation | custom fusion | bytes 2097216 | tf_op jit(solution)/shard_map/jit(_take)/gather | solution.py:35
  17.2 11.9 %all_gather.3 = bf16[1,2,128,1024]{3,2,1,0:T(8,128)(2,1)S(1)} all-gather(bf16[1,2,128,256]{3,2,1,0:T(8,128)(2,1)S(1)} %collective-permute-done), channel_id=1, replica_groups=mesh['pipe'=8,'dp'=32,'tensor'=4] {'tensor'}, dimensions={3}, use_global_device_ids=true | all-gather | bytes 655360 | tf_op jit(solution)/shard_map/all_gather | solution.py:19
  29.3 0.7 gather_fusion.1
  30.0 0.3 copy-done.1
  30.3 1.5 %fusion.13 = f32[16,128,128]{2,1,0:T(8,128)} fusion(bf16[16,256,128]{2,1,0:T(8,128)(2,1)S(1)} %gather_fusion.1, bf16[16,256,128]{2,1,0:T(8,128)(2,1)S(1)} %copy-done.1, pred[16]{0:T(512)(128)(4,1)S(1)} %get-tuple-element.11, pred[16]{0:T(512)(128)(4,1)S(1)} %get-tuple-element.12), kind=kOutput, calls=%fused_computation.16 | convolution fusion | flops 135266304 | bytes 3145760 | tf_op jit(solution)/shard_map/tmi,tmk->mik/dot_general | solution.py:38
  32.0 1.1 copy-done
  33.1 2.3 %abs_reduce_fusion = (f32[32,128]{1,0:T(8,128)S(1)}, f32[32,128,128]{2,0,1:T(8,128)S(1)}) fusion(s32[16]{0:T(128)S(1)} %fusion.26, f32[2,8,128,128]{3,2,1,0:T(8,128)S(1)} %convert.3, f32[2,8,128,128]{3,2,1,0:T(8,128)S(1)} %bitcast.95), kind=kOutput, calls=%fused_computation.8 | convolution fusion | flops 101970432 | bytes 4210752 | tf_op jit(solution)/shard_map/dot_general | solution.py:58
  35.4 0.6 maximum_multiply_fusion
  36.0 22.3 %all-to-all-start.2 = ((f32[32,1,128]{2,1,0:T(1,128)}), f32[32,1,128]{2,1,0:T(1,128)S(1)}, u32[]{:S(2)}, u32[]{:S(2)}) async-start(f32[32,1,128]{2,1,0:T(1,128)} %bitcast.15), calls=%async_computation.2 | async-start | bytes 32768 | tf_op jit(solution)/shard_map/all_to_all | solution.py:66
  58.3 0.4 round-nearest-even_convert_fusion
  58.7 1.4 %copy.66 = s16[32,128,128]{2,1,0:T(8,128)(2,1)} copy(s16[32,128,128]{2,0,1:T(8,128)(2,1)S(1)} %round-nearest-even_convert_fusion) | data formatting | bytes 2097152 | tf_op jit(solution)/shard_map/convert_element_type | solution.py:64
  60.1 10.0 %all-to-all-done.2 = f32[32,1,128]{2,1,0:T(1,128)S(1)} async-done(((f32[32,1,128]{2,1,0:T(1,128)}), f32[32,1,128]{2,1,0:T(1,128)S(1)}, u32[]{:S(2)}, u32[]{:S(2)}) %all-to-all-start.2) | async-done | bytes 16416 | tf_op jit(solution)/shard_map/all_to_all | solution.py:66
  70.1 4.5 %all-to-all-start.1 = ((s16[32,128,128]{2,1,0:T(8,128)(2,1)}), s16[32,128,128]{2,1,0:T(8,128)(2,1)S(1)}, u32[]{:S(2)}, u32[]{:S(2)}) async-start(s16[32,128,128]{2,1,0:T(8,128)(2,1)} %copy.66), calls=%async_computation.1 | async-start | bytes 2097152 | tf_op jit(solution)/shard_map/all_to_all | solution.py:65
  74.7 55.7 %all-to-all-done.1 = s16[32,128,128]{2,1,0:T(8,128)(2,1)S(1)} async-done(((s16[32,128,128]{2,1,0:T(8,128)(2,1)}), s16[32,128,128]{2,1,0:T(8,128)(2,1)S(1)}, u32[]{:S(2)}, u32[]{:S(2)}) %all-to-all-start.1) | async-done | bytes 1048608 | tf_op jit(solution)/shard_map/all_to_all | solution.py:65
  130.3 0.4 convert_multiply_fusion
  130.7 2.2 %fusion.6 = bf16[1,128,8,128]{3,2,1,0:T(8,128)(2,1)S(1)} fusion(f32[32,8]{0,1:T(8,128)S(1)} %convert_reduce_fusion, f32[4,8,128,128]{3,2,1,0:T(8,128)S(1)} %bitcast.89), kind=kOutput, calls=%fused_computation.10 | convolution fusion | flops 50462720 | bytes 2360320 | tf_op jit(solution)/shard_map/dot_general | solution.py:70
  132.9 0.8 convert_element_type.44
  (20 shorter events, 0.7 us)
Async XLA Ops:
  0.0 17.2 %collective-permute-start = (bf16[1,2,128,256]{3,2,1,0:T(8,128)(2,1)}, bf16[1,2,128,256]{3,2,1,0:T(8,128)(2,1)S(1)}, u32[]{:S(2)}, u32[]{:S(2)}) collective-permute-start(bf16[1,2,128,256]{3,2,1,0:T(8,128)(2,1)} %param.6), channel_id=1, source_target_pairs={{0,896},{128,0},{256,128},{384,256},{512,384},{640,512},{768,640},... | collective-permute-start | bytes 393224 | tf_op jit(solution)/shard_map/ppermute | solution.py:10
  5.9 26.0 %all-to-all-start = ((bf16[1,1,1,4,4,128,128]{6,5,4,2,1,0,3:T(8,128)(2,1)}), bf16[1,1,1,4,4,128,128]{6,5,4,2,1,0,3:T(8,128)(2,1)S(1)}, u32[]{:S(2)}, u32[]{:S(2)}) async-start(bf16[1,1,1,4,4,128,128]{6,5,4,2,1,0,3:T(8,128)(2,1)} %bitcast.96), calls=%async_computation | async-start | bytes 1048576 | tf_op jit(solution)/shard_map/all_to_all | solution.py:20
  29.1 1.2 copy-start.1
  31.9 1.2 copy-start
  36.0 34.0 %all-to-all-start.2 = ((f32[32,1,128]{2,1,0:T(1,128)}), f32[32,1,128]{2,1,0:T(1,128)S(1)}, u32[]{:S(2)}, u32[]{:S(2)}) async-start(f32[32,1,128]{2,1,0:T(1,128)} %bitcast.15), calls=%async_computation.2 | async-start | bytes 32768 | tf_op jit(solution)/shard_map/all_to_all | solution.py:66
  70.1 60.3 %all-to-all-start.1 = ((s16[32,128,128]{2,1,0:T(8,128)(2,1)}), s16[32,128,128]{2,1,0:T(8,128)(2,1)S(1)}, u32[]{:S(2)}, u32[]{:S(2)}) async-start(s16[32,128,128]{2,1,0:T(8,128)(2,1)} %copy.66), calls=%async_computation.1 | async-start | bytes 2097152 | tf_op jit(solution)/shard_map/all_to_all | solution.py:65

commit v2 on v0

v2 whole, which is shorter than its diff:
```python
import functools

import jax
import jax.numpy as jnp
from jax import lax
from jax.experimental import pallas as pl
from jax.experimental.pallas import tpu as pltpu
from jax.sharding import PartitionSpec as P

MESH = pl.DeviceIdType.MESH
LEVELS = 32767.0


def peer(index, place, chips, way):
    half = chips // 2
    turn = index + 2
    distance = half - turn // 4
    edge = (distance == half) | (distance == 0)
    flip = jnp.where(edge, (turn + 1) % 2, (turn // 2) % 2)
    sign = jnp.where(turn % 2 == 0, way, -way)
    chip = lax.rem(place // 2 + sign * distance + 2 * chips, chips)
    core = lax.rem(place % 2 + flip, 2)
    return chip * 2 + core


def kernel(
    rows, cols, picks, marks, activations, cotangent, errors, strip,
    held_in, held_out, held_err, codes_out, steps_out, codes_in, steps_in, total,
    in_sem, own_sem, pipe_sems, error_sems, column_sems, code_sems, step_sems,
):
    pipe_count, replicas = lax.axis_size("pipe"), lax.axis_size("dp")
    groups = lax.axis_size("tensor")
    chips = replicas // 2
    section, place, group = lax.axis_index("pipe"), lax.axis_index("dp"), lax.axis_index("tensor")
    before, after = lax.rem(section + pipe_count - 1, pipe_count), lax.rem(section + 1, pipe_count)
    right, left = lax.rem(group + 1, groups), lax.rem(group + groups - 1, groups)
    far = lax.rem(group + 2, groups)
    micro, tokens, width = cotangent.shape
    edge = codes_out.shape[-1]
    slots = errors.shape[1]
    blocks = width // edge

    def load_in(block):
        span = pl.ds(pl.multiple_of(block * edge, edge), edge)
        return pltpu.make_async_copy(
            activations.at[:, :, span], held_in.at[block], in_sem.at[block]
        )

    @pl.loop(0, held_in.shape[0])
    def _(block):
        load_in(block).start()

    def err_slots(origin):
        return held_err.at[pl.ds(origin * slots, slots)]

    load_err = pltpu.make_async_copy(errors.at[group], err_slots(group), own_sem)
    load_err.start()

    barrier = pltpu.get_barrier_semaphore()
    for name, other in (
        ("tensor", right), ("tensor", left), ("tensor", far), ("pipe", before), ("pipe", after),
    ):
        pl.semaphore_signal(barrier, inc=1, device_id={name: other}, device_id_type=MESH)

    @pl.loop(1, replicas)
    def _(step):
        other = lax.rem(place + step, replicas)
        pl.semaphore_signal(barrier, inc=1, device_id={"dp": other}, device_id_type=MESH)

    pl.semaphore_wait(barrier, replicas + 4)

    def remote(source, target, sems, slot, device):
        return pltpu.make_async_remote_copy(
            src_ref=source, dst_ref=target,
            send_sem=sems.at[(0,) + slot], recv_sem=sems.at[(1,) + slot],
            device_id=device, device_id_type=MESH,
        )

    def columns(origin, part):
        return held_out.at[pl.ds(origin * blocks, blocks), part]

    pipe_copies = []
    for part in range(micro):
        for block in range(blocks):
            copy = remote(
                cotangent.at[part, :, pl.ds(block * edge, edge)],
                held_out.at[group * blocks + block, part],
                pipe_sems, (part, block), {"pipe": before},
            )
            copy.start()
            pipe_copies.append(copy)
    error_copies = []
    for slot, other in enumerate((right, left, far)):
        copy = remote(
            errors.at[other], err_slots(group), error_sems, (slot,), {"tensor": other}
        )
        copy.start()
        error_copies.append(copy)

    to_right, to_left, onward = [], [], []
    for part in range(micro):
        for block in range(blocks):
            pipe_copies[part * blocks + block].wait_recv()
        own = columns(group, part)
        copy = remote(own, own, column_sems, (0, part), {"tensor": right})
        copy.start()
        to_right.append(copy)
        copy = remote(own, own, column_sems, (1, part), {"tensor": left})
        copy.start()
        to_left.append(copy)
    for part in range(micro):
        if part % 2 == 0:
            to_left[part].wait_recv()
            piece = columns(right, part)
            copy = remote(piece, piece, column_sems, (2, part), {"tensor": left})
        else:
            to_right[part].wait_recv()
            piece = columns(left, part)
            copy = remote(piece, piece, column_sems, (2, part), {"tensor": right})
        copy.start()
        onward.append(copy)

    @pl.loop(0, held_in.shape[0])
    def _(block):
        load_in(block).wait()

    load_err.wait()
    for copy in error_copies:
        copy.wait_recv()
    for part in range(micro):
        if part % 2 == 0:
            to_right[part].wait_recv()
        else:
            to_left[part].wait_recv()
    for copy in onward:
        copy.wait_recv()

    def exchange(index):
        other = peer(index, place, chips, 1)
        return (
            remote(codes_out.at[index], codes_in.at[index], code_sems, (index,), {"dp": other}),
            remote(steps_out.at[index], steps_in.at[index], step_sems, (index,), {"dp": other}),
        )

    def make_tile(index):
        other = peer(index, place, chips, 1)
        source = held_in[rows[other]].reshape(micro * tokens, edge)
        sink = held_out[cols[other]].reshape(micro * tokens, edge)
        tile = lax.dot_general(
            source, sink, (((0,), (0,)), ((), ())), preferred_element_type=jnp.float32
        )
        tile = tile + held_err[picks[other]].astype(jnp.float32)
        reach = jnp.maximum(jnp.max(jnp.abs(tile), axis=0, keepdims=True), 1e-30)
        codes = jnp.round(tile * (LEVELS / reach)).astype(jnp.int32)
        codes_out[index] = codes.astype(jnp.int16)
        steps_out[index] = reach * (1.0 / LEVELS)

    make_tile(0)

    @pl.loop(1, replicas)
    def _(index):
        make_tile(index)
        for copy in exchange(index - 1):
            copy.start()

    total[...] = jnp.zeros_like(total)

    def add_tile(index, codes, steps):
        mark = marks[peer(index, place, chips, -1)]
        value = codes[index].astype(jnp.int32).astype(jnp.float32) * steps[index]
        for block in range(total.shape[0]):
            total[block] += value * mark[block : block + 1]

    add_tile(replicas - 1, codes_out, steps_out)

    @pl.loop(0, replicas - 1)
    def _(index):
        for copy in exchange(index):
            copy.wait_recv()
        add_tile(index, codes_in, steps_in)

    for block in range(total.shape[0]):
        strip[:, pl.ds(block * edge, edge)] = total[block].astype(strip.dtype)

    for copy in pipe_copies + error_copies + to_right + to_left + onward:
        copy.wait_send()

    @pl.loop(0, replicas - 1)
    def _(index):
        for copy in exchange(index):
            copy.wait_send()


def tables(tile_picks, row_owners, blocks, lanes):
    replicas = tile_picks.shape[1]
    place = lax.axis_index("dp")
    groups, slots = tile_picks.shape[3:5]
    rows = tile_picks[0, :, 0, :, :, 0].reshape(replicas, groups * slots)
    offset = (jnp.arange(groups * slots, dtype=jnp.int32) // slots) * blocks
    cols = tile_picks[0, :, 0, :, :, 1].reshape(replicas, groups * slots) + offset
    owners = row_owners[0, 0]
    count = owners.shape[0]
    mine_rows = lax.dynamic_index_in_dim(rows, place, 0, keepdims=False)
    mine_cols = lax.dynamic_index_in_dim(cols, place, 0, keepdims=False)
    numbers = jnp.arange(count, dtype=jnp.int32)
    row_of = jnp.sum(jnp.where(owners[None, :] == numbers[:, None], numbers[None, :], 0), axis=1)
    picked = mine_rows[None, :] == row_of[:, None]
    numbers16 = jnp.arange(groups * slots, dtype=jnp.int32)

    def chosen(values):
        return jnp.sum(jnp.where(picked, values[None, :], 0), axis=1)

    my_row = jnp.sum(jnp.where(owners == place, numbers, 0))
    columns = jnp.arange(groups * blocks, dtype=jnp.int32)
    here = (rows == my_row)[..., None] & (cols[..., None] == columns)
    marks = jnp.sum(here.astype(jnp.float32), axis=1)
    marks = jnp.broadcast_to(marks[..., None], marks.shape + (lanes,))
    return chosen(mine_rows), chosen(mine_cols), chosen(numbers16), marks


def body(activations, cotangent, error_tiles, tile_picks, row_owners):
    edge = error_tiles.shape[-1]
    groups, replicas = lax.axis_size("tensor"), lax.axis_size("dp")
    micro, tokens, features = activations.shape[1:]
    width = cotangent.shape[-1]
    slots = error_tiles.shape[4]
    rows, cols, picks, marks = tables(tile_picks, row_owners, width // edge, edge)
    hbm = pl.BlockSpec(memory_space=pl.ANY)
    vmem, smem = pl.BlockSpec(memory_space=pltpu.VMEM), pl.BlockSpec(memory_space=pltpu.SMEM)
    dma = pltpu.SemaphoreType.DMA
    strip = pl.pallas_call(
        kernel,
        out_shape=jax.ShapeDtypeStruct((edge, groups * width), jnp.bfloat16),
        in_specs=[smem, smem, smem, vmem, hbm, hbm, hbm],
        out_specs=vmem,
        scratch_shapes=[
            pltpu.VMEM((features // edge, micro, tokens, edge), jnp.bfloat16),
            pltpu.VMEM((groups * width // edge, micro, tokens, edge), jnp.bfloat16),
            pltpu.VMEM((groups * slots, edge, edge), jnp.bfloat16),
            pltpu.VMEM((replicas, edge, edge), jnp.int16),
            pltpu.VMEM((replicas, 1, edge), jnp.float32),
            pltpu.VMEM((replicas, edge, edge), jnp.int16),
            pltpu.VMEM((replicas, 1, edge), jnp.float32),
            pltpu.VMEM((groups * width // edge, edge, edge), jnp.float32),
            dma((features // edge,)), dma(()), dma((2, micro, width // edge)),
            dma((2, 3)), dma((2, 3, micro)),
            dma((2, replicas)), dma((2, replicas)),
        ],
        compiler_params=pltpu.CompilerParams(
            collective_id=0, has_side_effects=True, vmem_limit_bytes=60 << 20
        ),
    )(
        rows, cols, picks, marks,
        activations.reshape(micro, tokens, features),
        cotangent.reshape(micro, tokens, width),
        error_tiles.reshape(groups, slots, edge, edge),
    )
    return strip.reshape(1, 1, edge, groups * width)


def solution(mesh):
    in_specs = (
        P("pipe", None, "dp", "tensor"),
        P("pipe", None, "dp", "tensor"),
        P("pipe", "dp", "tensor", None, None, None, None),
        P("pipe", None, "tensor", None, None, None),
        P("pipe", "tensor", None),
    )
    out_specs = P("pipe", "tensor", "dp", None)
    return jax.shard_map(body, mesh=mesh, in_specs=in_specs, out_specs=out_specs, check_vma=False)
```

time: 163 us -> 94.3 us (0.58)
  waiting for transfers between devices: 98.2 us -> 0 us
  Pallas kernels: 0 us -> 86.9 us
  starting transfers between devices: 32.3 us -> 0 us
  blocking collectives: 11.8 us -> 0 us
  local copies, waits for them, and re-layouts: 12 us -> 3.57 us
  matrix products: 6.32 us -> 0 us
  other arithmetic: 1.61 us -> 3.48 us
    all_to_all x2 -> x0, waiting for transfers between devices: 98.2 us -> none  [the longest x1 98.2 us: body(): lax.all_to_all(outgoing, 'dp', split_axis=0, concat_axis=0, tiled=True)]
    pallas_call x0 -> x1, Pallas kernels: none -> 86.9 us  [body(): pl.pallas_call(kernel, out_shape=jax.ShapeDtypeStruct((edge, groups * wid...]
    all_to_all x2 -> x0, starting transfers between devices: 26.4 us -> none  [the longest x1 22.4 us: body(): lax.all_to_all(outgoing, 'dp', split_axis=0, concat_axis=0, tiled=True)]
    all_gather x1 -> x0, blocking collectives: 11.8 us -> none  [body(): columns = lax.all_gather(returned, 'tensor', axis=3, tiled=True)]
    dot_general x3 -> x0, matrix products: 6.32 us -> none  [the longest x1 2.3 us: body(): jnp.dot(send_map, grads + carried, precision=highest, preferred_element_t...]
    ppermute x1 -> x0, starting transfers between devices: 5.9 us -> none  [passed_along(): return lax.ppermute(value, axis, pairs)]
    all_to_all x1 -> x0, local copies, waits for them, and re-layouts: 3.5 us -> none  [body(): lax.all_to_all(outgoing, 'dp', split_axis=0, concat_axis=0, tiled=True)]
    gather x2 -> x0, local copies, waits for them, and re-layouts: 3.38 us -> none  [the longest x1 1.71 us: body(): picked_in = jnp.take(inputs, mine_rows, axis=1)]
  transfers between devices with their start and end apart: 3 -> 0, of which waited for: 1 -> 0; matrix products, arithmetic and copies ran while one was open for 7% -> 0% of each run, Pallas kernels for 0% -> 0%
where the time goes in v2:
time: 94.3 us; the launch traced here: 94 us
  Pallas kernels  86.9 us (92%)
  local copies, waits for them, and re-layouts  3.57 us (4%)
  other arithmetic  3.48 us (4%)
    pallas_call x1, Pallas kernels, body(): pl.pallas_call(kernel, out_shape=jax.ShapeDtypeStruct((edge, groups * wid...  86.9 us

profile of v2, /device:TPU:1, one launch (start us, length us, event | category | flops | bytes accessed | tf_op | source)
XLA Modules:
  0.0 94.0 jit_solution(8720382535807023)
XLA Ops:
  0.0 1.3 %fusion.5 = s32[]{:T(128)} fusion(s32[]{:T(128)S(6)} %axis_index.15, s32[1,1,32]{2,1,0:T(1,128)} %param.9), kind=kLoop, calls=%fused_computation.20 | loop fusion | flops 95 | bytes 136 | tf_op jit(solution)/shard_map/reduce_sum | solution.py:213
  1.3 0.8 select_reduce_fusion
  2.1 0.8 fusion.6
  2.9 0.1 broadcast_add_fusion
  3.0 0.7 broadcast_compare_fusion
  3.6 0.2 dynamic-slice_reduce_fusion
  3.8 0.1 copy.17
  3.9 0.7 fusion.3
  4.6 0.1 copy.16
  4.6 0.8 broadcast_in_dim.64.marks
  5.4 86.9 %shard_map.55 = bf16[128,1024]{1,0:T(8,128)(2,1)} custom-call(s32[32]{0:T(128)} %get-tuple-element.7.rows, s32[32]{0:T(128)} %get-tuple-element.6.cols, s32[32]{0:T(128)} %get-tuple-element.5.picks, f32[32,8,128]{2,1,0:T(8,128)} %broadcast_in_dim.64.marks, bf16[2,128,4096]{2,1,0:T(8,128)(2,1)} %bitcast.9, bf16[2,128,256]{2,1,0:T(8,128)(2,1)} %bitcast.12, ...), custom_call_target="tpu_custom_call" | custom-call | tf_op jit(solution)/shard_map/pallas_call | solution.py:231
  92.3 1.7 %copy.19 = bf16[1,1,128,1024]{3,2,1,0:T(8,128)(2,1)} copy(bf16[1,1,128,1024]{3,2,1,0:T(8,128)(2,1)} %bitcast.10) | data formatting | bytes 524288
  (2 shorter events, 0.0 us)

commit v3 on v2

--- a/solution.py
+++ b/solution.py
@@ -1,5 +1,3 @@
-import functools
-
 import jax
 import jax.numpy as jnp
 from jax import lax
@@ -9,6 +7,11 @@
 
 MESH = pl.DeviceIdType.MESH
 LEVELS = 32767.0
+
+
+def hit(left, right):
+    apart = left - right
+    return 1 - jnp.minimum(apart * apart, 1)
 
 
 def peer(index, place, chips, way):
@@ -24,9 +27,9 @@
 
 
 def kernel(
-    rows, cols, picks, marks, activations, cotangent, errors, strip,
-    held_in, held_out, held_err, codes_out, steps_out, codes_in, steps_in, total,
-    in_sem, own_sem, pipe_sems, error_sems, column_sems, code_sems, step_sems,
+    picks, pick_scalars, owners, activations, cotangent, errors, strip,
+    held_in, held_out, held_err, codes_out, steps_out, codes_in, steps_in, listed, table,
+    in_sem, own_sem, table_sem, pipe_sems, error_sems, column_sems, code_sems, step_sems, near_sems,
 ):
     pipe_count, replicas = lax.axis_size("pipe"), lax.axis_size("dp")
     groups = lax.axis_size("tensor")
@@ -62,12 +65,37 @@
     ):
         pl.semaphore_signal(barrier, inc=1, device_id={name: other}, device_id_type=MESH)
 
-    @pl.loop(1, replicas)
-    def _(step):
-        other = lax.rem(place + step, replicas)
+    chip, core = place // 2, place % 2
+
+    def replica(shift, which):
+        return lax.rem(chip + shift + chips, chips) * 2 + which
+
+    near = [replica(shift, which) for shift in (1, -1) for which in (0, 1)]
+    for other in near + [replica(0, 1 - core)]:
         pl.semaphore_signal(barrier, inc=1, device_id={"dp": other}, device_id_type=MESH)
 
-    pl.semaphore_wait(barrier, replicas + 4)
+    rows = held_in.shape[0]
+    picked = groups * slots
+    lanes = lax.broadcasted_iota(jnp.int32, (1, replicas), 1)
+    row_of = jnp.zeros((1, replicas), jnp.int32)
+    my_row = 0
+    for row in range(rows):
+        row_of += hit(lanes, owners[row]) * row
+        my_row += hit(owners[row], place) * row
+    sends = jnp.zeros((1, replicas), jnp.int32)
+    hears = jnp.zeros((1, replicas), jnp.int32)
+    for pick in range(picked):
+        at = pick // slots, pick % slots
+        row = pick_scalars[at + (0, place)]
+        column = pick_scalars[at + (1, place)] + at[0] * blocks
+        sends += hit(row_of, row) * ((row * groups * blocks + column) * picked + pick)
+        hears += hit(picks[at + (pl.ds(0, 1),)], my_row) * (
+            picks[at + (pl.ds(1, 1),)] + (at[0] * blocks + 1)
+        )
+    listed[0:1, 0:replicas] = sends
+    listed[1:2, 0:replicas] = hears - 1
+
+    pl.semaphore_wait(barrier, 10)
 
     def remote(source, target, sems, slot, device):
         return pltpu.make_async_remote_copy(
@@ -97,6 +125,25 @@
         copy.start()
         error_copies.append(copy)
 
+    load_table = pltpu.make_async_copy(listed, table, table_sem)
+    load_table.start()
+
+    def meet(number):
+        distance = 2**number
+        for way, shift in enumerate((distance, -distance)):
+            for which in (0, 1):
+                pl.semaphore_signal(
+                    near_sems.at[number, way * 2 + core], inc=1,
+                    device_id={"dp": replica(shift, which)}, device_id_type=MESH,
+                )
+        for slot in range(4):
+            pl.semaphore_wait(near_sems.at[number, slot], 1)
+
+    meetings = near_sems.shape[0]
+    early = meetings - 1
+    for number in range(early):
+        meet(number)
+
     to_right, to_left, onward = [], [], []
     for part in range(micro):
         for block in range(blocks):
@@ -108,6 +155,8 @@
         copy = remote(own, own, column_sems, (1, part), {"tensor": left})
         copy.start()
         to_left.append(copy)
+    for number in range(early, meetings):
+        meet(number)
     for part in range(micro):
         if part % 2 == 0:
             to_left[part].wait_recv()
@@ -125,6 +174,7 @@
         load_in(block).wait()
 
     load_err.wait()
+    load_table.wait()
     for copy in error_copies:
         copy.wait_recv()
     for part in range(micro):
@@ -143,13 +193,15 @@
         )
 
     def make_tile(index):
-        other = peer(index, place, chips, 1)
-        source = held_in[rows[other]].reshape(micro * tokens, edge)
-        sink = held_out[cols[other]].reshape(micro * tokens, edge)
+        entry = table[0, peer(index, place, chips, 1)]
+        pick, entry = lax.rem(entry, picked), lax.div(entry, picked)
+        column, row = lax.rem(entry, groups * blocks), lax.div(entry, groups * blocks)
+        source = held_in[row].reshape(micro * tokens, edge)
+        sink = held_out[column].reshape(micro * tokens, edge)
         tile = lax.dot_general(
             source, sink, (((0,), (0,)), ((), ())), preferred_element_type=jnp.float32
         )
-        tile = tile + held_err[picks[other]].astype(jnp.float32)
+        tile = tile + held_err[pick].astype(jnp.float32)
         reach = jnp.maximum(jnp.max(jnp.abs(tile), axis=0, keepdims=True), 1e-30)
         codes = jnp.round(tile * (LEVELS / reach)).astype(jnp.int32)
         codes_out[index] = codes.astype(jnp.int16)
@@ -163,13 +215,14 @@
         for copy in exchange(index - 1):
             copy.start()
 
-    total[...] = jnp.zeros_like(total)
+    strip[...] = jnp.zeros_like(strip)
+    columns_at = lax.broadcasted_iota(jnp.int32, (groups * blocks, edge), 0)
 
     def add_tile(index, codes, steps):
-        mark = marks[peer(index, place, chips, -1)]
+        mark = hit(columns_at, table[1, peer(index, place, chips, -1)]).astype(jnp.float32)
         value = codes[index].astype(jnp.int32).astype(jnp.float32) * steps[index]
-        for block in range(total.shape[0]):
-            total[block] += value * mark[block : block + 1]
+        for block in range(groups * blocks):
+            strip[:, pl.ds(block * edge, edge)] += value * mark[block : block + 1]
 
     add_tile(replicas - 1, codes_out, steps_out)
 
@@ -179,9 +232,6 @@
             copy.wait_recv()
         add_tile(index, codes_in, steps_in)
 
-    for block in range(total.shape[0]):
-        strip[:, pl.ds(block * edge, edge)] = total[block].astype(strip.dtype)
-
     for copy in pipe_copies + error_copies + to_right + to_left + onward:
         copy.wait_send()
 
@@ -189,33 +239,6 @@
     def _(index):
         for copy in exchange(index):
             copy.wait_send()
-
-
-def tables(tile_picks, row_owners, blocks, lanes):
-    replicas = tile_picks.shape[1]
-    place = lax.axis_index("dp")
-    groups, slots = tile_picks.shape[3:5]
-    rows = tile_picks[0, :, 0, :, :, 0].reshape(replicas, groups * slots)
-    offset = (jnp.arange(groups * slots, dtype=jnp.int32) // slots) * blocks
-    cols = tile_picks[0, :, 0, :, :, 1].reshape(replicas, groups * slots) + offset
-    owners = row_owners[0, 0]
-    count = owners.shape[0]
-    mine_rows = lax.dynamic_index_in_dim(rows, place, 0, keepdims=False)
-    mine_cols = lax.dynamic_index_in_dim(cols, place, 0, keepdims=False)
-    numbers = jnp.arange(count, dtype=jnp.int32)
-    row_of = jnp.sum(jnp.where(owners[None, :] == numbers[:, None], numbers[None, :], 0), axis=1)
-    picked = mine_rows[None, :] == row_of[:, None]
-    numbers16 = jnp.arange(groups * slots, dtype=jnp.int32)
-
-    def chosen(values):
-        return jnp.sum(jnp.where(picked, values[None, :], 0), axis=1)
-
-    my_row = jnp.sum(jnp.where(owners == place, numbers, 0))
-    columns = jnp.arange(groups * blocks, dtype=jnp.int32)
-    here = (rows == my_row)[..., None] & (cols[..., None] == columns)
-    marks = jnp.sum(here.astype(jnp.float32), axis=1)
-    marks = jnp.broadcast_to(marks[..., None], marks.shape + (lanes,))
-    return chosen(mine_rows), chosen(mine_cols), chosen(numbers16), marks
 
 
 def body(activations, cotangent, error_tiles, tile_picks, row_owners):
@@ -224,14 +247,15 @@
     micro, tokens, features = activations.shape[1:]
     width = cotangent.shape[-1]
     slots = error_tiles.shape[4]
-    rows, cols, picks, marks = tables(tile_picks, row_owners, width // edge, edge)
+    picks = jnp.transpose(tile_picks[0, :, 0], (1, 2, 3, 0))
+    meetings = max(1, (replicas // 2 - 1).bit_length()) - 1
     hbm = pl.BlockSpec(memory_space=pl.ANY)
     vmem, smem = pl.BlockSpec(memory_space=pltpu.VMEM), pl.BlockSpec(memory_space=pltpu.SMEM)
     dma = pltpu.SemaphoreType.DMA
     strip = pl.pallas_call(
         kernel,
-        out_shape=jax.ShapeDtypeStruct((edge, groups * width), jnp.bfloat16),
-        in_specs=[smem, smem, smem, vmem, hbm, hbm, hbm],
+        out_shape=jax.ShapeDtypeStruct((edge, groups * width), jnp.float32),
+        in_specs=[vmem, smem, smem, hbm, hbm, hbm],
         out_specs=vmem,
         scratch_shapes=[
             pltpu.VMEM((features // edge, micro, tokens, edge), jnp.bfloat16),
@@ -241,21 +265,23 @@
             pltpu.VMEM((replicas, 1, edge), jnp.float32),
             pltpu.VMEM((replicas, edge, edge), jnp.int16),
             pltpu.VMEM((replicas, 1, edge), jnp.float32),
-            pltpu.VMEM((groups * width // edge, edge, edge), jnp.float32),
-            dma((features // edge,)), dma(()), dma((2, micro, width // edge)),
+            pltpu.VMEM((2, 128), jnp.int32),
+            pltpu.SMEM((2, 128), jnp.int32),
+            dma((features // edge,)), dma(()), dma(()), dma((2, micro, width // edge)),
             dma((2, 3)), dma((2, 3, micro)),
             dma((2, replicas)), dma((2, replicas)),
+            pltpu.SemaphoreType.REGULAR((max(1, meetings), 4)),
         ],
         compiler_params=pltpu.CompilerParams(
             collective_id=0, has_side_effects=True, vmem_limit_bytes=60 << 20
         ),
     )(
-        rows, cols, picks, marks,
+        picks, picks, row_owners[0, 0],
         activations.reshape(micro, tokens, features),
         cotangent.reshape(micro, tokens, width),
         error_tiles.reshape(groups, slots, edge, edge),
     )
-    return strip.reshape(1, 1, edge, groups * width)
+    return strip.astype(jnp.bfloat16).reshape(1, 1, edge, groups * width)
 
 
 def solution(mesh):

time: 94.3 us -> 88.1 us (0.934)
  local copies, waits for them, and re-layouts: 3.57 us -> 0 us
  other arithmetic: 3.48 us -> 1.78 us
  Pallas kernels: 86.9 us -> 85.8 us
    reduce_sum x4 -> x0, other arithmetic: 2.75 us -> none  [the longest x1 1.29 us: tables(): my_row = jnp.sum(jnp.where(owners == place, numbers, 0))]
    reshape x0 -> x1, other arithmetic: none -> 1.78 us  [body(): return strip.astype(jnp.bfloat16).reshape(1, 1, edge, groups * width)]
    unnamed x2 -> x0, local copies, waits for them, and re-layouts: 1.75 us -> none
    pallas_call x1, Pallas kernels: 86.9 us -> 85.8 us  [body(): pl.pallas_call(kernel, out_shape=jax.ShapeDtypeStruct((edge, groups * wid...]
where the time goes in v3:
time: 88.1 us; the launch traced here: 87.6 us
  Pallas kernels  85.8 us (97%)
  other arithmetic  1.78 us (2%)
    pallas_call x1, Pallas kernels, body(): pl.pallas_call(kernel, out_shape=jax.ShapeDtypeStruct((edge, groups * wid...  85.8 us
    reshape x1, other arithmetic, body(): return strip.astype(jnp.bfloat16).reshape(1, 1, edge, groups * width)  1.78 us

profile of v3, /device:TPU:1, one launch (start us, length us, event | category | flops | bytes accessed | tf_op | source)
XLA Modules:
  0.0 87.6 jit_solution(16178797020054703624)
XLA Ops:
  0.0 85.8 %shard_map.55 = f32[128,1024]{1,0:T(8,128)} custom-call(s32[4,4,2,32]{3,2,1,0:T(2,128)} %bitcast.12, s32[4,4,2,32]{3,2,1,0:T(2,128)} %bitcast.13, s32[32]{0:T(128)} %bitcast.14, bf16[2,128,4096]{2,1,0:T(8,128)(2,1)} %bitcast.9, bf16[2,128,256]{2,1,0:T(8,128)(2,1)} %bitcast.11, bf16[4,4,128,128]{3,2,1,0:T(8,128)(2,1)} %bitcast.10), custom_call_target="tpu_custom_call" | custom-call | tf_op jit(solution)/shard_map/pallas_call | solution.py:255
  85.8 1.8 %convert_bitcast_fusion = bf16[1,1,128,1024]{3,2,1,0:T(8,128)(2,1)} fusion(f32[128,1024]{1,0:T(8,128)} %shard_map.55), kind=kLoop, calls=%fused_computation | loop fusion | flops 131072 | bytes 786432 | tf_op jit(solution)/shard_map/reshape | solution.py:284

commit v4 on v3

v4 whole, which is shorter than its diff:
```python
import jax
import jax.numpy as jnp
from jax import lax
from jax.experimental import pallas as pl
from jax.experimental.pallas import tpu as pltpu
from jax.sharding import PartitionSpec as P

MESH = pl.DeviceIdType.MESH
LEVELS = 32767.0
RELAY = 2


def hit(left, right):
    apart = left - right
    return 1 - jnp.minimum(apart * apart, 1)


def kernel(
    picks, pick_scalars, owners, activations, cotangent, errors, strip,
    held_in, held_out, held_err, passing, codes_out, steps_out, codes_in, steps_in, sums, listed,
    table, in_sem, own_sem, table_sem, pipe_sems, error_sems, column_sems,
    code_send, code_recv, step_send, step_recv, near_sems,
):
    pipe_count, replicas = lax.axis_size("pipe"), lax.axis_size("dp")
    groups = lax.axis_size("tensor")
    chips = replicas // 2
    section, place, group = lax.axis_index("pipe"), lax.axis_index("dp"), lax.axis_index("tensor")
    before, after = lax.rem(section + pipe_count - 1, pipe_count), lax.rem(section + 1, pipe_count)
    right, left = lax.rem(group + 1, groups), lax.rem(group + groups - 1, groups)
    far = lax.rem(group + 2, groups)
    micro, tokens, width = cotangent.shape
    edge = codes_out.shape[-1]
    slots = errors.shape[1]
    blocks = width // edge

    def load_in(block):
        span = pl.ds(pl.multiple_of(block * edge, edge), edge)
        return pltpu.make_async_copy(
            activations.at[:, :, span], held_in.at[block], in_sem.at[block]
        )

    @pl.loop(0, held_in.shape[0])
    def _(block):
        load_in(block).start()

    picked = groups * slots
    first = slots // 2

    def err_slots(origin, start=0, count=slots):
        return held_err.at[pl.ds(origin * slots + start, count)]

    load_err = pltpu.make_async_copy(errors.at[group], err_slots(group), own_sem)
    load_err.start()

    barrier = pltpu.get_barrier_semaphore()
    for name, other in (
        ("tensor", right), ("tensor", left), ("tensor", far), ("pipe", before), ("pipe", after),
    ):
        pl.semaphore_signal(barrier, inc=1, device_id={name: other}, device_id_type=MESH)

    chip, core = place // 2, place % 2

    def replica(shift, which):
        return lax.rem(chip + shift + chips, chips) * 2 + which

    near = [replica(shift, which) for shift in (1, -1) for which in (0, 1)]
    for other in near + [replica(0, 1 - core)]:
        pl.semaphore_signal(barrier, inc=1, device_id={"dp": other}, device_id_type=MESH)

    pl.semaphore_wait(barrier, 10)

    def remote(source, target, sems, slot, device):
        return pltpu.make_async_remote_copy(
            src_ref=source, dst_ref=target,
            send_sem=sems.at[(0,) + slot], recv_sem=sems.at[(1,) + slot],
            device_id=device, device_id_type=MESH,
        )

    def columns(origin, part):
        return held_out.at[pl.ds(origin * blocks, blocks), part]

    pipe_copies = []
    for part in range(micro):
        for block in range(blocks):
            copy = remote(
                cotangent.at[part, :, pl.ds(block * edge, edge)],
                held_out.at[group * blocks + block, part],
                pipe_sems, (part, block), {"pipe": before},
            )
            copy.start()
            pipe_copies.append(copy)
    error_copies, through = [], []
    spans = (0, first), (first, slots - first)
    for way, other in enumerate((right, left)):
        start, count = spans[way]
        copy = remote(
            errors.at[far, pl.ds(start, count)], passing.at[pl.ds(start, count)],
            error_sems, (way,), {"tensor": other},
        )
        copy.start()
        through.append(copy)
    for way, other in enumerate((right, left)):
        copy = remote(
            errors.at[other], err_slots(group), error_sems, (2 + way,), {"tensor": other}
        )
        copy.start()
        error_copies.append(copy)

    def list_tables():
        lanes = lax.broadcasted_iota(jnp.int32, (1, replicas), 1)
        row_of = jnp.zeros((1, replicas), jnp.int32)
        owned = [place, replica(RELAY, core), replica(-RELAY, core)]
        wanted = [0 for _ in owned]
        for row in range(held_in.shape[0]):
            row_of += hit(lanes, owners[row]) * row
            wanted = [was + hit(owners[row], who) * row for was, who in zip(wanted, owned)]
        sends = jnp.zeros((1, replicas), jnp.int32)
        hears = [jnp.zeros((1, replicas), jnp.int32) for _ in owned]
        for pick in range(picked):
            at = pick // slots, pick % slots
            row = pick_scalars[at + (0, place)]
            column = pick_scalars[at + (1, place)] + at[0] * blocks
            sends += hit(row_of, row) * ((row * groups * blocks + column) * picked + pick)
            every_row = picks[at + (pl.ds(0, 1),)]
            every_column = picks[at + (pl.ds(1, 1),)] + (at[0] * blocks + 1)
            hears = [was + hit(every_row, row) * every_column for was, row in zip(hears, wanted)]
        listed[0:1, 0:replicas] = sends
        for number, columns in enumerate(hears):
            listed[number + 1 : number + 2, 0:replicas] = columns - 1

    def meet(number):
        distance = 2**number
        for way, shift in enumerate((distance, -distance)):
            for which in (0, 1):
                pl.semaphore_signal(
                    near_sems.at[number, way * 2 + core], inc=1,
                    device_id={"dp": replica(shift, which)}, device_id_type=MESH,
                )
        for slot in range(4):
            pl.semaphore_wait(near_sems.at[number, slot], 1)

    meetings = near_sems.shape[0]
    early = meetings - 1
    list_tables()
    for number in range(early):
        meet(number)
    load_table = pltpu.make_async_copy(listed, table, table_sem)
    load_table.start()
    for way, (origin, other) in enumerate(((left, right), (right, left))):
        start, count = spans[way]
        through[way].wait_recv()
        copy = remote(
            passing.at[pl.ds(start, count)], err_slots(origin, start, count),
            error_sems, (4 + way,), {"tensor": other},
        )
        copy.start()
        error_copies.append(copy)

    to_right, to_left, onward = [], [], []
    for part in range(micro):
        for block in range(blocks):
            pipe_copies[part * blocks + block].wait_recv()
        own = columns(group, part)
        copy = remote(own, own, column_sems, (0, part), {"tensor": right})
        copy.start()
        to_right.append(copy)
        copy = remote(own, own, column_sems, (1, part), {"tensor": left})
        copy.start()
        to_left.append(copy)
    for number in range(early, meetings):
        meet(number)
    for part in range(micro):
        if part % 2 == 0:
            to_left[part].wait_recv()
            piece = columns(right, part)
            copy = remote(piece, piece, column_sems, (2, part), {"tensor": left})
        else:
            to_right[part].wait_recv()
            piece = columns(left, part)
            copy = remote(piece, piece, column_sems, (2, part), {"tensor": right})
        copy.start()
        onward.append(copy)

    @pl.loop(0, held_in.shape[0])
    def _(block):
        load_in(block).wait()

    load_err.wait()
    load_table.wait()
    for copy in error_copies:
        copy.wait_recv()
    for part in range(micro):
        if part % 2 == 0:
            to_right[part].wait_recv()
        else:
            to_left[part].wait_recv()
    for copy in onward:
        copy.wait_recv()

    half = chips // 2
    gathered = 2 * (half - RELAY) - 1
    relayed = 2 * gathered
    direct_in = 2 * (gathered + 1)
    strips_in = direct_in + 5
    strips_out = replicas
    width_all = groups * blocks

    def post(source, target, device):
        return [
            pltpu.make_async_remote_copy(
                src_ref=out.at[source], dst_ref=into.at[target],
                send_sem=send.at[source], recv_sem=recv.at[target],
                device_id={"dp": device}, device_id_type=MESH,
            )
            for out, into, send, recv in (
                (codes_out, codes_in, code_send, code_recv),
                (steps_out, steps_in, step_send, step_recv),
            )
        ]

    def far_tile(index):
        turn = index + 2
        distance = half - turn // 4
        across = distance == half
        flip = jnp.where(across, turn % 2, (turn // 2) % 2)
        side = jnp.where(across, core, turn % 2)
        way = 1 - 2 * side
        which = lax.rem(core + flip, 2)
        slot = jnp.where(across, 0, 1 + (half - 1 - distance) * 2 + flip)
        return (
            replica(way * distance, which), replica(way * (distance - RELAY), which),
            side * (gathered + 1) + slot,
        )

    near_tiles = []
    for side, way in enumerate((1, -1)):
        near_tiles.append((
            replica(way * RELAY, 1 - core), replica(0, 1 - core), side * (gathered + 1) + gathered
        ))
    for side, way in enumerate((1, -1)):
        near_tiles.append((replica(way * RELAY, core), None, None))
    for flip in (0, 1):
        for side, way in enumerate((1, -1)):
            which = lax.rem(core + flip, 2)
            other = replica(way, which)
            near_tiles.append((other, other, direct_in + side * 2 + flip))
    other = replica(0, 1 - core)
    near_tiles.append((other, other, direct_in + 4))
    near_tiles.append((place, None, None))
    kept = relayed + 2

    def encode(value, slot):
        reach = jnp.maximum(jnp.max(jnp.abs(value), axis=0, keepdims=True), 1e-30)
        codes = jnp.round(value * (LEVELS / reach)).astype(jnp.int32)
        codes_out[slot] = codes.astype(jnp.int16)
        steps_out[slot] = reach * (1.0 / LEVELS)

    def decode(codes, steps, slot):
        return codes[slot].astype(jnp.int32).astype(jnp.float32) * steps[slot]

    def make_tile(index, target):
        entry = table[0, target]
        pick, entry = lax.rem(entry, picked), lax.div(entry, picked)
        column, row = lax.rem(entry, width_all), lax.div(entry, width_all)
        source = held_in[row].reshape(micro * tokens, edge)
        sink = held_out[column].reshape(micro * tokens, edge)
        tile = lax.dot_general(
            source, sink, (((0,), (0,)), ((), ())), preferred_element_type=jnp.float32
        )
        encode(tile + held_err[pick].astype(jnp.float32), index)

    def send_far(index):
        _, gatherer, slot = far_tile(index)
        return post(index, slot, gatherer)

    make_tile(0, far_tile(0)[0])

    @pl.loop(1, relayed)
    def _(index):
        make_tile(index, far_tile(index)[0])
        for copy in send_far(index - 1):
            copy.start()

    waiting = send_far(relayed - 1)
    sent = []
    for number, (target, device, slot) in enumerate(near_tiles):
        make_tile(relayed + number, target)
        for copy in waiting:
            copy.start()
        waiting = post(relayed + number, slot, device) if slot is not None else []
        sent += waiting
    for copy in waiting:
        copy.start()

    columns_at = lax.broadcasted_iota(jnp.int32, (width_all, edge), 0)
    sums[...] = jnp.zeros_like(sums)

    def await_slot(slot):
        for copy in post(0, slot, place):
            copy.wait_recv()

    def add_tile(number, source, codes, steps, slot):
        mark = hit(columns_at, table[1 + number, source]).astype(jnp.float32)
        value = decode(codes, steps, slot)
        for block in range(width_all):
            sums[number, :, pl.ds(block * edge, edge)] += value * mark[block : block + 1]

    sides = (1, 0), (2, 1)
    for number, side in sides:
        add_tile(number, place, codes_out, steps_out, kept + side)
        slot = side * (gathered + 1) + gathered
        await_slot(slot)
        add_tile(number, replica(0, 1 - core), codes_in, steps_in, slot)
    for number, side in sides:
        slot = side * (gathered + 1)
        await_slot(slot)
        source = replica((2 * side - 1) * (half - RELAY), side)
        add_tile(number, source, codes_in, steps_in, slot)

    @pl.loop(0, gathered - 1)
    def _(index):
        distance = half - 1 - index // 2
        which = lax.rem(core + index % 2, 2)
        for number, side in sides:
            slot = side * (gathered + 1) + 1 + index
            await_slot(slot)
            source = replica((2 * side - 1) * (distance - RELAY), which)
            add_tile(number, source, codes_in, steps_in, slot)

    waiting = []
    for block in range(width_all):
        for number, side in sides:
            spot = side * width_all + block
            encode(sums[number, :, pl.ds(block * edge, edge)], strips_out + spot)
            for copy in waiting:
                copy.start()
            device = replica((1 - 2 * side) * RELAY, core)
            waiting = post(strips_out + spot, strips_in + spot, device)
            sent += waiting
    for copy in waiting:
        copy.start()

    add_tile(0, place, codes_out, steps_out, replicas - 1)
    await_slot(direct_in + 4)
    add_tile(0, replica(0, 1 - core), codes_in, steps_in, direct_in + 4)
    for flip in (0, 1):
        for side in (0, 1):
            slot = direct_in + side * 2 + flip
            await_slot(slot)
            source = replica(2 * side - 1, lax.rem(core + flip, 2))
            add_tile(0, source, codes_in, steps_in, slot)
    for block in range(width_all):
        span = pl.ds(block * edge, edge)
        value = sums[0, :, span]
        for side in (0, 1):
            slot = strips_in + side * width_all + block
            await_slot(slot)
            value = value + decode(codes_in, steps_in, slot)
        strip[:, span] = value.astype(strip.dtype)

    for copy in pipe_copies + through + error_copies + to_right + to_left + onward + sent:
        copy.wait_send()

    @pl.loop(0, relayed)
    def _(index):
        for copy in send_far(index):
            copy.wait_send()


def body(activations, cotangent, error_tiles, tile_picks, row_owners):
    edge = error_tiles.shape[-1]
    groups, replicas = lax.axis_size("tensor"), lax.axis_size("dp")
    micro, tokens, features = activations.shape[1:]
    width = cotangent.shape[-1]
    slots = error_tiles.shape[4]
    picks = jnp.transpose(tile_picks[0, :, 0], (1, 2, 3, 0))
    strips = 2 * groups * width // edge
    outbox = replicas + strips
    inbox = 4 * (replicas // 4 - RELAY) + 5 + strips
    meetings = max(1, (replicas // 2 - 1).bit_length()) - 1
    hbm = pl.BlockSpec(memory_space=pl.ANY)
    vmem, smem = pl.BlockSpec(memory_space=pltpu.VMEM), pl.BlockSpec(memory_space=pltpu.SMEM)
    dma = pltpu.SemaphoreType.DMA
    strip = pl.pallas_call(
        kernel,
        out_shape=jax.ShapeDtypeStruct((edge, groups * width), jnp.bfloat16),
        in_specs=[vmem, smem, smem, hbm, hbm, hbm],
        out_specs=vmem,
        scratch_shapes=[
            pltpu.VMEM((features // edge, micro, tokens, edge), jnp.bfloat16),
            pltpu.VMEM((groups * width // edge, micro, tokens, edge), jnp.bfloat16),
            pltpu.VMEM((groups * slots, edge, edge), jnp.bfloat16),
            pltpu.VMEM((slots, edge, edge), jnp.bfloat16),
            pltpu.VMEM((outbox, edge, edge), jnp.int16),
            pltpu.VMEM((outbox, 1, edge), jnp.float32),
            pltpu.VMEM((inbox, edge, edge), jnp.int16),
            pltpu.VMEM((inbox, 1, edge), jnp.float32),
            pltpu.VMEM((3, edge, groups * width), jnp.float32),
            pltpu.VMEM((4, 128), jnp.int32),
            pltpu.SMEM((4, 128), jnp.int32),
            dma((features // edge,)), dma(()), dma(()), dma((2, micro, width // edge)),
            dma((2, 6)), dma((2, 3, micro)),
            dma((outbox,)), dma((inbox,)), dma((outbox,)), dma((inbox,)),
            pltpu.SemaphoreType.REGULAR((max(1, meetings), 4)),
        ],
        compiler_params=pltpu.CompilerParams(
            collective_id=0, has_side_effects=True, vmem_limit_bytes=60 << 20
        ),
    )(
        picks, picks, row_owners[0, 0],
        activations.reshape(micro, tokens, features),
        cotangent.reshape(micro, tokens, width),
        error_tiles.reshape(groups, slots, edge, edge),
    )
    return strip.reshape(1, 1, edge, groups * width)


def solution(mesh):
    in_specs = (
        P("pipe", None, "dp", "tensor"),
        P("pipe", None, "dp", "tensor"),
        P("pipe", "dp", "tensor", None, None, None, None),
        P("pipe", None, "tensor", None, None, None),
        P("pipe", "tensor", None),
    )
    out_specs = P("pipe", "tensor", "dp", None)
    return jax.shard_map(body, mesh=mesh, in_specs=in_specs, out_specs=out_specs, check_vma=False)
```

time: 88.1 us -> 82.5 us (0.936)
  Pallas kernels: 85.8 us -> 80.5 us
  other arithmetic: 1.78 us -> 0 us
  local copies, waits for them, and re-layouts: 0 us -> 1.67 us
    pallas_call x1, Pallas kernels: 85.8 us -> 80.5 us  [body(): pl.pallas_call(kernel, out_shape=jax.ShapeDtypeStruct((edge, groups * wid...]
    reshape x1 -> x0, other arithmetic: 1.78 us -> none  [body(): return strip.astype(jnp.bfloat16).reshape(1, 1, edge, groups * width)]
    unnamed x0 -> x1, local copies, waits for them, and re-layouts: none -> 1.67 us
where the time goes in v4:
time: 82.5 us; the launch traced here: 82.2 us
  Pallas kernels  80.5 us (98%)
  local copies, waits for them, and re-layouts  1.67 us (2%)
    pallas_call x1, Pallas kernels, body(): pl.pallas_call(kernel, out_shape=jax.ShapeDtypeStruct((edge, groups * wid...  80.5 us
    unnamed x1, local copies, waits for them, and re-layouts  1.67 us

profile of v4, /device:TPU:1, one launch (start us, length us, event | category | flops | bytes accessed | tf_op | source)
XLA Modules:
  0.0 82.2 jit_solution(14989562209156798914)
XLA Ops:
  0.0 80.5 %shard_map.55 = bf16[128,1024]{1,0:T(8,128)(2,1)} custom-call(s32[4,4,2,32]{3,2,1,0:T(2,128)} %bitcast.12, s32[4,4,2,32]{3,2,1,0:T(2,128)} %bitcast.13, s32[32]{0:T(128)} %bitcast.14, bf16[2,128,4096]{2,1,0:T(8,128)(2,1)} %bitcast.8, bf16[2,128,256]{2,1,0:T(8,128)(2,1)} %bitcast.11, bf16[4,4,128,128]{3,2,1,0:T(8,128)(2,1)} %bitcast.10), custom_call_target="tpu_custom_call" | custom-call | tf_op jit(solution)/shard_map/pallas_call | solution.py:384
  80.5 1.7 %copy.7 = bf16[1,1,128,1024]{3,2,1,0:T(8,128)(2,1)} copy(bf16[1,1,128,1024]{3,2,1,0:T(8,128)(2,1)} %bitcast.9) | data formatting | bytes 524288

commit v5 on v4

--- a/solution.py
+++ b/solution.py
@@ -16,9 +16,10 @@
 
 
 def kernel(
-    picks, pick_scalars, owners, activations, cotangent, errors, strip,
+    all_picks, all_owners, activations, cotangent, errors, strip,
+    picks, pick_scalars, owners, rounded,
     held_in, held_out, held_err, passing, codes_out, steps_out, codes_in, steps_in, sums, listed,
-    table, in_sem, own_sem, table_sem, pipe_sems, error_sems, column_sems,
+    table, list_sems, out_sems, in_sem, own_sem, table_sem, pipe_sems, error_sems, column_sems,
     code_send, code_recv, step_send, step_recv, near_sems,
 ):
     pipe_count, replicas = lax.axis_size("pipe"), lax.axis_size("dp")
@@ -39,22 +40,15 @@
             activations.at[:, :, span], held_in.at[block], in_sem.at[block]
         )
 
-    @pl.loop(0, held_in.shape[0])
-    def _(block):
-        load_in(block).start()
-
     picked = groups * slots
     first = slots // 2
 
     def err_slots(origin, start=0, count=slots):
         return held_err.at[pl.ds(origin * slots + start, count)]
 
-    load_err = pltpu.make_async_copy(errors.at[group], err_slots(group), own_sem)
-    load_err.start()
-
     barrier = pltpu.get_barrier_semaphore()
     for name, other in (
-        ("tensor", right), ("tensor", left), ("tensor", far), ("pipe", before), ("pipe", after),
+        ("tensor", right), ("tensor", left), ("pipe", before), ("pipe", after),
     ):
         pl.semaphore_signal(barrier, inc=1, device_id={name: other}, device_id_type=MESH)
 
@@ -67,7 +61,15 @@
     for other in near + [replica(0, 1 - core)]:
         pl.semaphore_signal(barrier, inc=1, device_id={"dp": other}, device_id_type=MESH)
 
-    pl.semaphore_wait(barrier, 10)
+    list_loads = [
+        pltpu.make_async_copy(source, target, list_sems.at[number])
+        for number, (source, target) in enumerate(
+            ((all_picks, picks), (all_picks, pick_scalars), (all_owners, owners))
+        )
+    ]
+    for copy in list_loads:
+        copy.start()
+    pl.semaphore_wait(barrier, 9)
 
     def remote(source, target, sems, slot, device):
         return pltpu.make_async_remote_copy(
@@ -105,6 +107,13 @@
         )
         copy.start()
         error_copies.append(copy)
+
+    @pl.loop(0, held_in.shape[0])
+    def _(block):
+        load_in(block).start()
+
+    load_err = pltpu.make_async_copy(errors.at[group], err_slots(group), own_sem)
+    load_err.start()
 
     def list_tables():
         lanes = lax.broadcasted_iota(jnp.int32, (1, replicas), 1)
@@ -141,6 +150,8 @@
 
     meetings = near_sems.shape[0]
     early = meetings - 1
+    for copy in list_loads:
+        copy.wait()
     list_tables()
     for number in range(early):
         meet(number)
@@ -340,6 +351,11 @@
     for copy in waiting:
         copy.start()
 
+    def store(block):
+        return pltpu.make_async_copy(
+            rounded.at[block], strip.at[:, pl.ds(block * edge, edge)], out_sems.at[block]
+        )
+
     add_tile(0, place, codes_out, steps_out, replicas - 1)
     await_slot(direct_in + 4)
     add_tile(0, replica(0, 1 - core), codes_in, steps_in, direct_in + 4)
@@ -356,7 +372,10 @@
             slot = strips_in + side * width_all + block
             await_slot(slot)
             value = value + decode(codes_in, steps_in, slot)
-        strip[:, span] = value.astype(strip.dtype)
+        rounded[block] = value.astype(strip.dtype)
+        if block > 0:
+            store(block - 1).start()
+    store(width_all - 1).start()
 
     for copy in pipe_copies + through + error_copies + to_right + to_left + onward + sent:
         copy.wait_send()
@@ -365,6 +384,9 @@
     def _(index):
         for copy in send_far(index):
             copy.wait_send()
+
+    for block in range(width_all):
+        store(block).wait()
 
 
 def body(activations, cotangent, error_tiles, tile_picks, row_owners):
@@ -379,14 +401,17 @@
     inbox = 4 * (replicas // 4 - RELAY) + 5 + strips
     meetings = max(1, (replicas // 2 - 1).bit_length()) - 1
     hbm = pl.BlockSpec(memory_space=pl.ANY)
-    vmem, smem = pl.BlockSpec(memory_space=pltpu.VMEM), pl.BlockSpec(memory_space=pltpu.SMEM)
     dma = pltpu.SemaphoreType.DMA
     strip = pl.pallas_call(
         kernel,
         out_shape=jax.ShapeDtypeStruct((edge, groups * width), jnp.bfloat16),
-        in_specs=[vmem, smem, smem, hbm, hbm, hbm],
-        out_specs=vmem,
+        in_specs=[hbm] * 5,
+        out_specs=hbm,
         scratch_shapes=[
+            pltpu.VMEM(picks.shape, jnp.int32),
+            pltpu.SMEM(picks.shape, jnp.int32),
+            pltpu.SMEM(row_owners.shape[2:], jnp.int32),
+            pltpu.VMEM((groups * width // edge, edge, edge), jnp.bfloat16),
             pltpu.VMEM((features // edge, micro, tokens, edge), jnp.bfloat16),
             pltpu.VMEM((groups * width // edge, micro, tokens, edge), jnp.bfloat16),
             pltpu.VMEM((groups * slots, edge, edge), jnp.bfloat16),
@@ -398,6 +423,7 @@
             pltpu.VMEM((3, edge, groups * width), jnp.float32),
             pltpu.VMEM((4, 128), jnp.int32),
             pltpu.SMEM((4, 128), jnp.int32),
+            dma((3,)), dma((groups * width // edge,)),
             dma((features // edge,)), dma(()), dma(()), dma((2, micro, width // edge)),
             dma((2, 6)), dma((2, 3, micro)),
             dma((outbox,)), dma((inbox,)), dma((outbox,)), dma((inbox,)),
@@ -407,7 +433,7 @@
             collective_id=0, has_side_effects=True, vmem_limit_bytes=60 << 20
         ),
     )(
-        picks, picks, row_owners[0, 0],
+        picks, row_owners[0, 0],
         activations.reshape(micro, tokens, features),
         cotangent.reshape(micro, tokens, width),
         error_tiles.reshape(groups, slots, edge, edge),

time: 82.5 us -> 81.4 us (0.987)
  Pallas kernels: 80.5 us -> 79.5 us
    pallas_call x1, Pallas kernels: 80.5 us -> 79.5 us  [body(): pl.pallas_call(kernel, out_shape=jax.ShapeDtypeStruct((edge, groups * wid...]
where the time goes in v5:
time: 81.4 us; the launch traced here: 81.2 us
  Pallas kernels  79.5 us (98%)
  local copies, waits for them, and re-layouts  1.67 us (2%)
    pallas_call x1, Pallas kernels, body(): pl.pallas_call(kernel, out_shape=jax.ShapeDtypeStruct((edge, groups * wid...  79.5 us
    unnamed x1, local copies, waits for them, and re-layouts  1.67 us

profile of v5, /device:TPU:1, one launch (start us, length us, event | category | flops | bytes accessed | tf_op | source)
XLA Modules:
  0.0 81.2 jit_solution(2190667482185263114)
XLA Ops:
  0.0 79.5 %shard_map.55 = bf16[128,1024]{1,0:T(8,128)(2,1)} custom-call(s32[4,4,2,32]{3,2,1,0:T(2,128)} %bitcast.12, s32[32]{0:T(128)} %bitcast.13, bf16[2,128,4096]{2,1,0:T(8,128)(2,1)} %bitcast.8, bf16[2,128,256]{2,1,0:T(8,128)(2,1)} %bitcast.11, bf16[4,4,128,128]{3,2,1,0:T(8,128)(2,1)} %bitcast.10), custom_call_target="tpu_custom_call" | custom-call | tf_op jit(solution)/shard_map/pallas_call | solution.py:405
  79.6 1.7 %copy.7 = bf16[1,1,128,1024]{3,2,1,0:T(8,128)(2,1)} copy(bf16[1,1,128,1024]{3,2,1,0:T(8,128)(2,1)} %bitcast.9) | data formatting | bytes 524288

commit v6 on v5

--- a/solution.py
+++ b/solution.py
@@ -19,7 +19,7 @@
     all_picks, all_owners, activations, cotangent, errors, strip,
     picks, pick_scalars, owners, rounded,
     held_in, held_out, held_err, passing, codes_out, steps_out, codes_in, steps_in, sums, listed,
-    table, list_sems, out_sems, in_sem, own_sem, table_sem, pipe_sems, error_sems, column_sems,
+    table, list_sems, out_sems, in_sem, own_sem, table_sem, pipe_sems, far_sems, error_sems, column_sems,
     code_send, code_recv, step_send, step_recv, near_sems,
 ):
     pipe_count, replicas = lax.axis_size("pipe"), lax.axis_size("dp")
@@ -51,6 +51,10 @@
         ("tensor", right), ("tensor", left), ("pipe", before), ("pipe", after),
     ):
         pl.semaphore_signal(barrier, inc=1, device_id={name: other}, device_id_type=MESH)
+    for other in (before, after):
+        pl.semaphore_signal(
+            barrier, inc=1, device_id={"pipe": other, "tensor": far}, device_id_type=MESH
+        )
 
     chip, core = place // 2, place % 2
 
@@ -69,7 +73,7 @@
     ]
     for copy in list_loads:
         copy.start()
-    pl.semaphore_wait(barrier, 9)
+    pl.semaphore_wait(barrier, 11)
 
     def remote(source, target, sems, slot, device):
         return pltpu.make_async_remote_copy(
@@ -91,6 +95,16 @@
             )
             copy.start()
             pipe_copies.append(copy)
+    onward = []
+    for part in range(micro):
+        for block in range(blocks):
+            copy = remote(
+                cotangent.at[part, :, pl.ds(block * edge, edge)],
+                held_out.at[group * blocks + block, part],
+                far_sems, (part, block), {"pipe": before, "tensor": far},
+            )
+            copy.start()
+            onward.append(copy)
     error_copies, through = [], []
     spans = (0, first), (first, slots - first)
     for way, other in enumerate((right, left)):
@@ -167,7 +181,7 @@
         copy.start()
         error_copies.append(copy)
 
-    to_right, to_left, onward = [], [], []
+    to_right, to_left = [], []
     for part in range(micro):
         for block in range(blocks):
             pipe_copies[part * blocks + block].wait_recv()
@@ -180,18 +194,6 @@
         to_left.append(copy)
     for number in range(early, meetings):
         meet(number)
-    for part in range(micro):
-        if part % 2 == 0:
-            to_left[part].wait_recv()
-            piece = columns(right, part)
-            copy = remote(piece, piece, column_sems, (2, part), {"tensor": left})
-        else:
-            to_right[part].wait_recv()
-            piece = columns(left, part)
-            copy = remote(piece, piece, column_sems, (2, part), {"tensor": right})
-        copy.start()
-        onward.append(copy)
-
     @pl.loop(0, held_in.shape[0])
     def _(block):
         load_in(block).wait()
@@ -200,12 +202,7 @@
     load_table.wait()
     for copy in error_copies:
         copy.wait_recv()
-    for part in range(micro):
-        if part % 2 == 0:
-            to_right[part].wait_recv()
-        else:
-            to_left[part].wait_recv()
-    for copy in onward:
+    for copy in to_right + to_left + onward:
         copy.wait_recv()
 
     half = chips // 2
@@ -424,8 +421,8 @@
             pltpu.VMEM((4, 128), jnp.int32),
             pltpu.SMEM((4, 128), jnp.int32),
             dma((3,)), dma((groups * width // edge,)),
-            dma((features // edge,)), dma(()), dma(()), dma((2, micro, width // edge)),
-            dma((2, 6)), dma((2, 3, micro)),
+            dma((features // edge,)), dma(()), dma(()), dma((2, micro, width // edge)), dma((2, micro, width // edge)),
+            dma((2, 6)), dma((2, 2, micro)),
             dma((outbox,)), dma((inbox,)), dma((outbox,)), dma((inbox,)),
             pltpu.SemaphoreType.REGULAR((max(1, meetings), 4)),
         ],

time: 81.4 us -> 81.5 us (level)
  no operation moved by 1% of the time
where the time goes in v6:
time: 81.5 us; the launch traced here: 81.3 us
  Pallas kernels  79.6 us (98%)
  local copies, waits for them, and re-layouts  1.67 us (2%)
    pallas_call x1, Pallas kernels, body(): pl.pallas_call(kernel, out_shape=jax.ShapeDtypeStruct((edge, groups * wid...  79.6 us
    unnamed x1, local copies, waits for them, and re-layouts  1.67 us

profile of v6, /device:TPU:1, one launch (start us, length us, event | category | flops | bytes accessed | tf_op | source)
XLA Modules:
  0.0 81.3 jit_solution(7542026428944901610)
XLA Ops:
  0.0 79.6 %shard_map.55 = bf16[128,1024]{1,0:T(8,128)(2,1)} custom-call(s32[4,4,2,32]{3,2,1,0:T(2,128)} %bitcast.12, s32[32]{0:T(128)} %bitcast.13, bf16[2,128,4096]{2,1,0:T(8,128)(2,1)} %bitcast.8, bf16[2,128,256]{2,1,0:T(8,128)(2,1)} %bitcast.11, bf16[4,4,128,128]{3,2,1,0:T(8,128)(2,1)} %bitcast.10), custom_call_target="tpu_custom_call" | custom-call | tf_op jit(solution)/shard_map/pallas_call | solution.py:402
  79.6 1.7 %copy.7 = bf16[1,1,128,1024]{3,2,1,0:T(8,128)(2,1)} copy(bf16[1,1,128,1024]{3,2,1,0:T(8,128)(2,1)} %bitcast.9) | data formatting | bytes 524288
